TPU v7x, 32 devices: a whole 2x2x4 slice. The times are simulated.
32 devices in a mesh: replica: 4 (over y, x), fsdp: 2 (over core), tensor: 4 (over z).
Axes of the slice: x: 2, y: 2, z: 4, core: 2. Of those that a mesh axis runs over, the one named last changes fastest.
Arguments:
- attn_out: bfloat16 [2048, 8192], P(('replica', 'tensor'), 'fsdp'), may hold values from -6 to 6
- out_grad: bfloat16 [2048, 8192], P(('replica', 'fsdp'), 'tensor'), may hold values from -0.25 to 0.25
- error_in: float32 [4, 8192, 8192], P('replica', 'fsdp', 'tensor'), may hold values from -4 to 4
- factor_in: float32 [8192, 32], P('tensor'), may hold values from -0.0625 to 0.0625
Outputs:
- new_error: float32 [4, 8192, 8192], P('replica', 'fsdp', 'tensor')
- update: bfloat16 [8192, 8192], P('fsdp', 'tensor')
- new_factor: float32 [8192, 32], P('tensor')
All inputs are finite; a program needn't handle non-finite values.
Results may differ from a plain program's by a relative error of at most 0.001.
Values may be sent and summed in bfloat16 or wider, within the bound.
A program may use at most 128 MiB of HBM per device.

v0:
```python
import jax
import jax.numpy as jnp
from jax import lax
from jax.sharding import PartitionSpec as P


def fold_rows(out_grad, activations, memory):
    return memory + lax.dot_general(
        activations,
        lax.all_gather(out_grad, "fsdp", axis=0, tiled=True),
        (((0,), (0,)), ((), ())),
        preferred_element_type=jnp.float32,
    )


def orthonormalize(partial_left, replicas):
    left = lax.psum(partial_left, ("replica", "tensor")) / replicas
    gram_local = jnp.dot(left.T, left, precision=lax.Precision.HIGHEST)
    gram_matrix = lax.psum(gram_local, "fsdp")
    triangle = jnp.linalg.cholesky(gram_matrix)
    return jax.scipy.linalg.solve_triangular(triangle, left.T, lower=True).T


def body(attn_out, out_grad, error_in, factor_in):
    activations = lax.all_gather(attn_out, "tensor", axis=0, tiled=True)
    replicas = lax.axis_size("replica")
    projected = jnp.dot(out_grad.astype(jnp.float32), factor_in, precision=lax.Precision.HIGHEST)
    projected_all = lax.all_gather(projected, "fsdp", axis=0, tiled=True)
    partial_left = lax.dot_general(
        activations,
        projected_all,
        (((0,), (0,)), ((), ())),
        precision=lax.Precision.HIGHEST,
        preferred_element_type=jnp.float32,
    )
    partial_left = partial_left + jnp.dot(error_in[0], factor_in, precision=lax.Precision.HIGHEST)
    orthonormal = orthonormalize(partial_left, replicas)
    merged = fold_rows(out_grad, activations, error_in[0])
    factor_local = lax.dot_general(
        merged, orthonormal, (((0,), (0,)), ((), ())), precision=lax.Precision.HIGHEST
    )
    new_factor = lax.psum(factor_local, ("replica", "fsdp")) / replicas
    decompressed = jnp.dot(orthonormal, new_factor.T, precision=lax.Precision.HIGHEST)
    new_error = (merged - decompressed)[None]
    return (new_error, decompressed.astype(jnp.bfloat16), new_factor)


def solution(mesh):
    placed = (
        P(("replica", "tensor"), "fsdp"),
        P(("replica", "fsdp"), "tensor"),
        P("replica", "fsdp", "tensor"),
        P("tensor", None),
    )
    return jax.shard_map(
        body,
        mesh=mesh,
        in_specs=placed,
        out_specs=(P("replica", "fsdp", "tensor"), P("fsdp", "tensor"), P("tensor", None)),
        check_vma=False,
    )
```

profile of v0, /device:TPU:0, one launch (start us, length us, event | category | flops | bytes accessed | tf_op | source)
XLA Modules:
  0.0 355.7 jit_solution(17522907834601763414)
XLA Ops:
  7.2 0.0 copy-start
  7.2 0.0 all-gather.3.cloned.1.call-start
  7.2 0.7 all-gather.3.cloned.1.call-update
  7.9 0.0 all-gather.5.cloned.1.call-start
  8.0 0.7 all-gather.5.cloned.1.call-update
  8.7 0.0 all-reduce.3.cloned.1.call-start
  8.7 0.0 copy-done
  8.7 2.2 fusion.15
  10.9 2.1 all_gather.11
  13.0 34.1 %fusion = f32[4096,32]{0,1:T(8,128)S(1)} fusion(f32[2048,32]{0,1:T(8,128)S(1)} %copy-done, f32[1,4096,2048]{2,1,0:T(8,128)} %param.6), kind=kOutput, calls=%fused_computation | convolution fusion | flops 3221225472 | bytes 34340864 | tf_op jit(solution)/shard_map/dot_general | solution.py:36
  47.2 45.9 %all-gather.3.cloned.1.call-done = bf16[512,4096]{1,0:T(8,128)(2,1)} async-done(((bf16[128,4096]{1,0:T(8,128)(2,1)}), bf16[512,4096]{1,0:T(8,128)(2,1)}) %all-gather.3.cloned.1.call-update) | async-done | bytes 4194320 | tf_op jit(solution)/shard_map/all_gather | solution.py:25
  93.1 5.2 %fusion.2 = f32[4096,32]{0,1:T(8,128)} fusion(f32[4096,32]{0,1:T(8,128)S(1)} %fusion, f32[512,32]{1,0:T(8,128)S(1)} %all_gather.11, bf16[512,4096]{1,0:T(8,128)(2,1)} %all-gather.3.cloned.1.call-done), kind=kOutput, calls=%fused_computation.5 | convolution fusion | flops 805437440 | bytes 5308416 | tf_op jit(solution)/shard_map/dot_general | solution.py:29
  98.3 0.0 all-reduce.3.cloned.1.call-update
  98.3 0.2 all-reduce.5.cloned.1.call-start
  98.5 5.2 %all-gather.5.cloned.1.call-done = bf16[512,2048]{1,0:T(8,128)(2,1)} async-done(((bf16[256,2048]{1,0:T(8,128)(2,1)}), bf16[512,2048]{1,0:T(8,128)(2,1)}) %all-gather.5.cloned.1.call-update) | async-done | bytes 2097168 | tf_op jit(solution)/shard_map/all_gather | solution.py:10
  103.7 28.3 %bitcast_add_fusion = f32[4096,2048]{1,0:T(8,128)} fusion(f32[1,4096,2048]{2,1,0:T(8,128)} %param.6, bf16[512,4096]{1,0:T(8,128)(2,1)} %all-gather.3.cloned.1.call-done, bf16[512,2048]{1,0:T(8,128)(2,1)} %all-gather.5.cloned.1.call-done), kind=kOutput, calls=%fused_computation.2 | convolution fusion | flops 8598323200 | bytes 73400320 | tf_op jit(solution)/shard_map/dot_general | solution.py:8
  132.0 87.7 %all-reduce.3.cloned.1.call-done = f32[4096,32]{0,1:T(8,128)} async-done(((f32[4096,32]{0,1:T(8,128)}), f32[4096,32]{0,1:T(8,128)}) %all-reduce.3.cloned.1.call-update) | async-done | bytes 524304 | tf_op jit(solution)/shard_map/psum | solution.py:17
  219.7 1.8 fusion.5
  221.6 3.4 psum.22
  224.9 0.1 copy.8
  225.0 2.9 cholesky.16
  228.0 0.6 compare_reduce_fusion
  228.6 0.7 fusion.9
  229.3 2.4 custom-call.7
  231.7 1.7 fusion.3
  233.4 24.4 %fusion.16 = f32[2048,32]{0,1:T(8,128)} fusion(f32[4096,2048]{1,0:T(8,128)} %bitcast_add_fusion, f32[32,4096]{1,0:T(8,128)S(1)} %fusion.3), kind=kOutput, calls=%fused_computation.26 | convolution fusion | flops 3221225472 | bytes 34340864 | tf_op jit(solution)/shard_map/dot_general | solution.py:39
  257.8 0.0 all-reduce.5.cloned.1.call-update
  257.8 53.0 %all-reduce.5.cloned.1.call-done = f32[2048,32]{0,1:T(8,128)} async-done(((f32[2048,32]{0,1:T(8,128)}), f32[2048,32]{0,1:T(8,128)}) %all-reduce.5.cloned.1.call-update) | async-done | bytes 262160 | tf_op jit(solution)/shard_map/psum | solution.py:42
  310.8 1.0 broadcast_multiply_fusion
  311.9 0.0 copy-start.2
  311.9 37.2 %fusion.14 = (bf16[4096,2048]{1,0:T(8,128)(2,1)}, f32[1,4096,2048]{2,1,0:T(8,128)}) fusion(f32[4096,2048]{1,0:T(8,128)} %bitcast_add_fusion, f32[32,4096]{1,0:T(8,128)S(1)} %fusion.3, f32[2048,32]{0,1:T(8,128)S(1)} %broadcast_multiply_fusion), kind=kOutput, calls=%fused_computation.24 | convolution fusion | flops 3238002688 | bytes 84672512 | tf_op jit(solution)/shard_map/dot_general | solution.py:43
  349.1 0.0 copy-done.2
  (4 shorter events, 0.0 us)
Async XLA Ops:
  7.2 1.5 copy-start
  7.2 85.9 %all-gather.3.cloned.1.call-start = ((), (), s32[]{:S(2)}) async-start(), calls=%async_computation | async-start | bytes 5242880 | tf_op jit(solution)/shard_map/all_gather | solution.py:25
  7.9 95.8 %all-gather.5.cloned.1.call-start = ((), (), s32[]{:S(2)}) async-start(), calls=%async_computation.1 | async-start | bytes 3145728 | tf_op jit(solution)/shard_map/all_gather | solution.py:10
  8.7 211.1 %all-reduce.3.cloned.1.call-start = ((), (), s32[]{:S(2)}) async-start(), calls=%async_computation.2 | async-start | bytes 1048576 | tf_op jit(solution)/shard_map/psum | solution.py:17
  98.3 212.5 %all-reduce.5.cloned.1.call-start = ((), (), s32[]{:S(2)}) async-start(), calls=%async_computation.3 | async-start | bytes 524288 | tf_op jit(solution)/shard_map/psum | solution.py:42
  310.8 38.3 %copy-start.1 = (f32[2048,32]{0,1:T(8,128)S(1)}, f32[2048,32]{0,1:T(8,128)}, u32[]{:S(2)}) copy-start(f32[2048,32]{0,1:T(8,128)} %param.7) | copy-start | bytes 786436
  311.9 37.3 %copy-start.2 = (f32[2048,32]{0,1:T(8,128)}, f32[2048,32]{0,1:T(8,128)S(1)}, u32[]{:S(2)}) copy-start(f32[2048,32]{0,1:T(8,128)S(1)} %broadcast_multiply_fusion) | copy-start | bytes 786436
Sparse Core Ops, SparseCore 0:
  9.6 83.4 all-gather.2
  94.6 9.0 all-gather.4
  109.4 110.2 all-reduce.2
  257.9 52.8 all-reduce.4
where the time goes:
time: 356 us
  waiting for transfers between devices  193 us (54%)
  matrix products  135 us (38%)
  between operations  13.8 us (4%)
  other arithmetic  7.7 us (2%)
  blocking collectives  5.48 us (2%)
    psum x1, waiting for transfers between devices, orthonormalize(): left = lax.psum(partial_left, ('replica', 'tensor')) / replicas  87.7 us
    psum x1, waiting for transfers between devices, body(): new_factor = lax.psum(factor_local, ('replica', 'fsdp')) / replicas  53 us
    all_gather x1, waiting for transfers between devices, body(): activations = lax.all_gather(attn_out, 'tensor', axis=0, tiled=True)  45.9 us
    dot_general x1, matrix products, body(): jnp.dot(orthonormal, new_factor.T, precision=lax.Precision.HIGHEST)  37.2 us
    dot_general x1, matrix products, body(): jnp.dot(error_in[0], factor_in, precision=lax.Precision.HIGHEST)  34.1 us
    dot_general x1, matrix products, fold_rows(): lax.dot_general(activations, lax.all_gather(out_grad, 'fsdp', axis=0, til...  28.3 us
    dot_general x1, matrix products, body(): lax.dot_general(merged, orthonormal, (((0,), (0,)), ((), ())), precision=...  24.4 us
  transfers between devices with their start and end apart: 4, of which 4 were waited for; matrix products, arithmetic and copies ran while one was open for 20% of the time, Pallas kernels for 0%

commit v1 on v0

--- a/solution.py
+++ b/solution.py
@@ -22,7 +22,19 @@
 
 
 def body(attn_out, out_grad, error_in, factor_in):
-    activations = lax.all_gather(attn_out, "tensor", axis=0, tiled=True)
+    devs = lax.axis_size("tensor")
+    row_list = [attn_out]
+    h = 0
+    while h < devs - 1:
+        row_list.append(
+            lax.ppermute(row_list[-1], "tensor", [(s, (s + 1) % devs) for s in range(devs)])
+        )
+        h = h + 1
+    activations = jnp.roll(
+        jnp.concatenate(row_list[::-1], axis=0),
+        (lax.axis_index("tensor") + 1) * attn_out.shape[0],
+        axis=0,
+    )
     replicas = lax.axis_size("replica")
     projected = jnp.dot(out_grad.astype(jnp.float32), factor_in, precision=lax.Precision.HIGHEST)
     projected_all = lax.all_gather(projected, "fsdp", axis=0, tiled=True)

time: 356 us -> 350 us (0.983)
  waiting for transfers between devices: 193 us -> 181 us
  local copies, waits for them, and re-layouts: 0.1 us -> 4.16 us
    ppermute x0 -> x3, waiting for transfers between devices: none -> 47.1 us  [body(): lax.ppermute(row_list[-1], 'tensor', [(s, (s + 1) % devs) for s in range(...]
    all_gather x1 -> x0, waiting for transfers between devices: 45.9 us -> none  [body(): activations = lax.all_gather(attn_out, 'tensor', axis=0, tiled=True)]
    psum x1, waiting for transfers between devices: 87.7 us -> 81.1 us  [orthonormalize(): left = lax.psum(partial_left, ('replica', 'tensor')) / replicas]
    all_gather x1, waiting for transfers between devices: 5.16 us -> 0.02 us  [fold_rows(): lax.all_gather(out_grad, 'fsdp', axis=0, tiled=True)]
    unnamed x6 -> x19, local copies, waits for them, and re-layouts: 0.02 us -> 4.02 us
  transfers between devices with their start and end apart: 4 -> 6, of which waited for: 4 -> 4; matrix products, arithmetic and copies ran while one was open for 20% -> 20% of each run, Pallas kernels for 0% -> 0%
where the time goes in v1:
time: 350 us
  waiting for transfers between devices  181 us (52%)
  matrix products  133 us (38%)
  between operations  15.7 us (4%)
  other arithmetic  7.66 us (2%)
  blocking collectives  5.49 us (2%)
  local copies, waits for them, and re-layouts  4.16 us (1%)
    psum x1, waiting for transfers between devices, orthonormalize(): left = lax.psum(partial_left, ('replica', 'tensor')) / replicas  81.1 us
    psum x1, waiting for transfers between devices, body(): new_factor = lax.psum(factor_local, ('replica', 'fsdp')) / replicas  52.5 us
    ppermute x3, waiting for transfers between devices, body(): lax.ppermute(row_list[-1], 'tensor', [(s, (s + 1) % devs) for s in range(...  47.1 us
    dot_general x1, matrix products, body(): jnp.dot(orthonormal, new_factor.T, precision=lax.Precision.HIGHEST)  37.3 us
    dot_general x1, matrix products, body(): jnp.dot(error_in[0], factor_in, precision=lax.Precision.HIGHEST)  34.1 us
    dot_general x1, matrix products, fold_rows(): lax.dot_general(activations, lax.all_gather(out_grad, 'fsdp', axis=0, til...  28.4 us
    dot_general x1, matrix products, body(): lax.dot_general(merged, orthonormal, (((0,), (0,)), ((), ())), precision=...  24.4 us
  transfers between devices with their start and end apart: 6, of which 4 were waited for; matrix products, arithmetic and copies ran while one was open for 20% of the time, Pallas kernels for 0%

profile of v1, /device:TPU:0, one launch (start us, length us, event | category | flops | bytes accessed | tf_op | source)
XLA Modules:
  0.0 350.1 jit_solution(3396239112371096186)
XLA Ops:
  8.1 3.1 collective-permute-start
  11.2 25.4 %collective-permute-done = bf16[128,4096]{1,0:T(8,128)(2,1)S(1)} collective-permute-done((bf16[128,4096]{1,0:T(8,128)(2,1)}, bf16[128,4096]{1,0:T(8,128)(2,1)S(1)}, u32[]{:S(2)}, u32[]{:S(2)}) %collective-permute-start) | collective-permute-done | bytes 1048608 | tf_op jit(solution)/shard_map/ppermute | solution.py:30
  36.6 0.0 all-reduce.3.cloned.1.call-start
  36.7 2.2 fusion.18
  38.9 2.1 all_gather.7
  41.0 21.7 %collective-permute-done.1 = bf16[128,4096]{1,0:T(8,128)(2,1)S(1)} collective-permute-done((bf16[128,4096]{1,0:T(8,128)(2,1)S(1)}, bf16[128,4096]{1,0:T(8,128)(2,1)S(1)}, u32[]{:S(2)}, u32[]{:S(2)}) %collective-permute-start.1) | collective-permute-done | bytes 1048608 | tf_op jit(solution)/shard_map/ppermute | solution.py:30
  62.7 34.1 %fusion = f32[4096,32]{0,1:T(8,128)S(1)} fusion(f32[2048,32]{0,1:T(8,128)S(1)} %copy-done, f32[1,4096,2048]{2,1,0:T(8,128)} %param.6), kind=kOutput, calls=%fused_computation | convolution fusion | flops 3221225472 | bytes 34340864 | tf_op jit(solution)/shard_map/dot_general | solution.py:48
  96.9 0.1 constant_dynamic-update-slice_fusion.7
  97.0 0.1 constant_dynamic-update-slice_fusion.6
  97.0 0.1 constant_dynamic-update-slice_fusion.5
  97.2 0.1 constant_dynamic-update-slice_fusion.4
  97.2 0.1 constant_dynamic-update-slice_fusion.3
  97.3 0.1 constant_dynamic-update-slice_fusion.2
  97.4 0.1 constant_dynamic-update-slice_fusion.1
  97.5 0.1 constant_dynamic-update-slice_fusion
  97.6 3.4 copy-done.2
  101.0 3.1 convolution_add_fusion
  104.1 0.2 all-reduce.5.cloned.1.call-start
  104.4 28.4 %bitcast_add_fusion = f32[4096,2048]{1,0:T(8,128)} fusion(f32[1,4096,2048]{2,1,0:T(8,128)} %param.6, bf16[512,2048]{1,0:T(8,128)(2,1)} %all-gather.2.cloned.1.call-done, bf16[1024,4096]{1,0:T(8,128)(2,1)} %copy-done.2, s32[]{:T(128)S(6)} %select_n.18), kind=kOutput, calls=%fused_computation.2 | convolution fusion | flops 8598323200 | bytes 73400320 | tf_op jit(solution)/shard_map/dot_general | solution.py:8
  132.8 81.1 %all-reduce.3.cloned.1.call-done = f32[4096,32]{0,1:T(8,128)} async-done(((f32[4096,32]{0,1:T(8,128)}), f32[4096,32]{0,1:T(8,128)}) %all-reduce.3.cloned.1.call-update) | async-done | bytes 524304 | tf_op jit(solution)/shard_map/psum | solution.py:17
  213.8 1.8 fusion.6
  215.6 3.4 psum.22
  219.0 0.1 copy.8
  219.1 2.9 cholesky.16
  222.0 0.6 compare_reduce_fusion
  222.7 0.7 fusion.10
  223.3 2.4 custom-call.7
  225.8 1.7 fusion.4
  227.4 24.4 %fusion.19 = f32[2048,32]{0,1:T(8,128)} fusion(f32[4096,2048]{1,0:T(8,128)} %bitcast_add_fusion, f32[32,4096]{1,0:T(8,128)S(1)} %fusion.4), kind=kOutput, calls=%fused_computation.37 | convolution fusion | flops 3221225472 | bytes 34340864 | tf_op jit(solution)/shard_map/dot_general | solution.py:51
  251.9 52.5 %all-reduce.5.cloned.1.call-done = f32[2048,32]{0,1:T(8,128)} async-done(((f32[2048,32]{0,1:T(8,128)}), f32[2048,32]{0,1:T(8,128)}) %all-reduce.5.cloned.1.call-update) | async-done | bytes 262160 | tf_op jit(solution)/shard_map/psum | solution.py:54
  304.4 1.0 broadcast_multiply_fusion
  305.4 37.3 %fusion.17 = (bf16[4096,2048]{1,0:T(8,128)(2,1)}, f32[1,4096,2048]{2,1,0:T(8,128)}) fusion(f32[4096,2048]{1,0:T(8,128)} %bitcast_add_fusion, f32[32,4096]{1,0:T(8,128)S(1)} %fusion.4, f32[2048,32]{0,1:T(8,128)S(1)} %broadcast_multiply_fusion), kind=kOutput, calls=%fused_computation.35 | convolution fusion | flops 3238002688 | bytes 84672512 | tf_op jit(solution)/shard_map/dot_general | solution.py:55
  (21 shorter events, 0.2 us)
Async XLA Ops:
  8.0 28.7 %copy-start = (f32[2048,32]{0,1:T(8,128)S(1)}, f32[2048,32]{0,1:T(8,128)}, u32[]{:S(2)}) copy-start(f32[2048,32]{0,1:T(8,128)} %param.7) | copy-start | bytes 786436
  8.0 96.3 %all-gather.2.cloned.1.call-start = ((), (), s32[]{:S(2)}) async-start(), calls=%async_computation | async-start | bytes 3145728 | tf_op jit(solution)/shard_map/all_gather | solution.py:10
  8.1 28.5 %collective-permute-start = (bf16[128,4096]{1,0:T(8,128)(2,1)}, bf16[128,4096]{1,0:T(8,128)(2,1)S(1)}, u32[]{:S(2)}, u32[]{:S(2)}) collective-permute-start(bf16[128,4096]{1,0:T(8,128)(2,1)} %param.4), channel_id=1, source_target_pairs={{0,1},{1,2},{2,3},{3,0},{4,5},{5,6},{6,7},{7,4},{8,9},{9,10},{10,1... | collective-permute-start | bytes 3145736 | tf_op jit(solution)/shard_map/ppermute | solution.py:30
  36.6 26.1 %collective-permute-start.1 = (bf16[128,4096]{1,0:T(8,128)(2,1)S(1)}, bf16[128,4096]{1,0:T(8,128)(2,1)S(1)}, u32[]{:S(2)}, u32[]{:S(2)}) collective-permute-start(bf16[128,4096]{1,0:T(8,128)(2,1)S(1)} %collective-permute-done), channel_id=1, source_target_pairs={{0,1},{1,2},{2,3},{3,0},{4,5},{5,6},{6,7},{7,4},{8,9},{9,10},{10,1... | collective-permute-start | bytes 3145736 | tf_op jit(solution)/shard_map/ppermute | solution.py:30
  36.6 177.2 %all-reduce.3.cloned.1.call-start = ((), (), s32[]{:S(2)}) async-start(), calls=%async_computation.1 | async-start | bytes 1048576 | tf_op jit(solution)/shard_map/psum | solution.py:17
  41.0 56.2 %copy-start.3 = (bf16[128,4096]{1,0:T(8,128)(2,1)S(1)}, bf16[128,4096]{1,0:T(8,128)(2,1)}, u32[]{:S(2)}) copy-start(bf16[128,4096]{1,0:T(8,128)(2,1)} %param.4) | copy-start | bytes 3145732
  62.7 34.2 %collective-permute-start.2 = (bf16[128,4096]{1,0:T(8,128)(2,1)S(1)}, bf16[128,4096]{1,0:T(8,128)(2,1)S(1)}, u32[]{:S(2)}, u32[]{:S(2)}) collective-permute-start(bf16[128,4096]{1,0:T(8,128)(2,1)S(1)} %collective-permute-done.1), channel_id=1, source_target_pairs={{0,1},{1,2},{2,3},{3,0},{4,5},{5,6},{6,7},{7,4},{8,9},{9,10},{10,1... | collective-permute-start | bytes 3145736 | tf_op jit(solution)/shard_map/ppermute | solution.py:30
  96.8 4.2 %copy-start.5 = (f32[512,32]{1,0:T(8,128)S(1)}, f32[512,32]{1,0:T(8,128)}, u32[]{:S(2)}) copy-start(f32[512,32]{1,0:T(8,128)} %all_gather.7) | copy-start | bytes 196612
  97.6 3.4 copy-start.2
  104.1 200.3 %all-reduce.5.cloned.1.call-start = ((), (), s32[]{:S(2)}) async-start(), calls=%async_computation.2 | async-start | bytes 524288 | tf_op jit(solution)/shard_map/psum | solution.py:54
  305.3 37.3 %copy-start.4 = (f32[2048,32]{0,1:T(8,128)}, f32[2048,32]{0,1:T(8,128)S(1)}, u32[]{:S(2)}) copy-start(f32[2048,32]{0,1:T(8,128)S(1)} %broadcast_multiply_fusion) | copy-start | bytes 786436
  305.4 37.3 %copy-start.1 = (f32[2048,32]{0,1:T(8,128)S(1)}, f32[2048,32]{0,1:T(8,128)}, u32[]{:S(2)}) copy-start(f32[2048,32]{0,1:T(8,128)} %param.7) | copy-start | bytes 786436
Sparse Core Ops, SparseCore 0:
  36.7 12.0 all-gather.1
Sparse Core Ops, SparseCore 1:
  104.2 109.6 all-reduce.2
  252.0 52.4 all-reduce.4
